TPU v7x, 32 devices: a whole 2x2x4 slice. The times are simulated.
32 devices in a mesh: dp: 4 (over x, core), group: 4 (over z), tensor: 2 (over y).
Axes of the slice: x: 2, y: 2, z: 4, core: 2. Of those that a mesh axis runs over, the one named last changes fastest.
Arguments:
- residual_in: bfloat16 [32, 1024, 767], P(('dp', 'group'), 'tensor'), may hold values from -6 to 6
- piece_ids: int32 [32, 1024], P(('dp', 'group')), may hold values from -1 to 3, as said below
- norm_gains: bfloat16 [2, 768], replicated, may hold values from 0.25 to 1.75
- qkv_weight: bfloat16 [3, 768, 768], P(None, None, 'tensor'), may hold values from -0.21875 to 0.21875
- qv_bias: bfloat16 [2, 768], P(None, 'tensor'), may hold values from -3 to 3
- out_weight: bfloat16 [768, 767], P('tensor'), may hold values from -0.875 to 0.875
- fc_weight: bfloat16 [768, 3072], P(None, 'tensor'), may hold values from -0.21875 to 0.21875
- fc_bias: bfloat16 [3072], P('tensor'), may hold values from -3 to 3
- proj_weight: bfloat16 [3072, 767], P('tensor'), may hold values from -0.109375 to 0.109375
- out_biases: bfloat16 [2, 767], replicated, may hold values from -2 to 2
- cotangent: bfloat16 [32, 1024, 767], P(('dp', 'group'), 'tensor'), may hold values from -6 to 6
Outputs:
- block_out: bfloat16 [32, 1024, 767], P(('dp', 'group'), 'tensor')
- grad_input: bfloat16 [32, 1024, 767], P(('dp', 'group'), 'tensor')
- grad_gains: float32 [2, 768], replicated
- grad_qkv: float32 [3, 768, 768], P(None, 'dp', 'tensor')
- grad_qv_bias: float32 [2, 768], P(None, ('tensor', 'dp'))
- grad_out_weight: float32 [768, 767], P(('tensor', 'dp'))
- grad_fc_weight: float32 [768, 3072], P('dp', 'tensor')
- grad_fc_bias: float32 [3072], P(('tensor', 'dp'))
- grad_proj_weight: float32 [3072, 767], P(('tensor', 'dp'))
- grad_out_biases: float32 [2, 767], replicated
Inputs may be any that keep to these rules, and one draw needn't show every extreme that they name: `piece_ids`: each aligned block of 256 positions of a sequence carries one id: -1 (text) or the block's own number (a picture piece). The first block of every sequence is text and the last one a picture piece.
All inputs are finite; a program needn't handle non-finite values.
Results may differ from a plain program's by a relative error of at most 0.02.
Values may be sent and summed in bfloat16 or wider, within the bound.
No kernel may reach another device: no remote copies, remote signals or barrier semaphores. Data moves between devices by JAX's collectives and lax.ppermute only.
A program may use at most 192 MiB of HBM per device.

v0:
```python
import jax
import jax.numpy as jnp
from jax import lax
from jax.sharding import PartitionSpec as P

D = 768
HD = 64
EPSILON = 1e-05
MASKED = -1e30


def decompress(compact):
    return jnp.concatenate([compact, -jnp.sum(compact, axis=-1, keepdims=True)], axis=-1)


def crms_gain(compact, gain):
    full_rows = decompress(compact)
    factor = lax.rsqrt(jnp.mean(full_rows * full_rows, axis=-1, keepdims=True) + EPSILON)
    return full_rows * factor * gain


def gelu_tanh(values):
    return jax.nn.gelu(values, approximate=True)


def visible_mask(labels, row_start, row_count):
    query_pos = row_start + jnp.arange(row_count)
    key_pos = jnp.arange(labels.shape[0])
    row_labels = labels[row_start : row_start + row_count]
    causal = key_pos[None, :] <= query_pos[:, None]
    inside = (row_labels[:, None] == labels[None, :]) & (row_labels[:, None] >= 0)
    return causal | inside


def block_scores(row_query, key_rows, labels, row_start, row_block):
    scores = jnp.einsum(
        "qhd,khd->hqk", row_query, key_rows, preferred_element_type=jnp.float32
    ) * HD ** (-0.5)
    return jnp.where(visible_mask(labels, row_start, row_block)[None], scores, MASKED)


def attend_forward(inputs):
    queries, key_rows, value_rows, labels = inputs
    length = key_rows.shape[0]
    row_block = min(512, length)
    outputs = []
    log_parts = []
    for row_start in range(0, length, row_block):
        scores = block_scores(
            queries[row_start : row_start + row_block], key_rows, labels, row_start, row_block
        )
        highest = jnp.max(scores, axis=-1, keepdims=True)
        weights = jnp.exp(scores - highest)
        weight_sum = jnp.sum(weights, axis=-1, keepdims=True)
        prob_low = (weights / weight_sum).astype(jnp.bfloat16)
        outputs.append(
            jnp.einsum(
                "hqk,khd->qhd", prob_low, value_rows, preferred_element_type=jnp.float32
            ).astype(jnp.bfloat16)
        )
        log_parts.append((highest + jnp.log(weight_sum))[..., 0])
    return (jnp.concatenate(outputs, 0), jnp.concatenate(log_parts, 1))


def attend_backward(inputs):
    queries, key_rows, value_rows, labels, upstream, log_sums = inputs
    length = key_rows.shape[0]
    row_block = min(512, length)
    score_scale = HD ** (-0.5)
    grad_keys = jnp.zeros(key_rows.shape, jnp.float32)
    grad_values = jnp.zeros(value_rows.shape, jnp.float32)
    query_grads = []
    for row_start in range(0, length, row_block):
        row_query = queries[row_start : row_start + row_block]
        row_up = upstream[row_start : row_start + row_block]
        scores = block_scores(row_query, key_rows, labels, row_start, row_block)
        probs = jnp.exp(scores - log_sums[:, row_start : row_start + row_block, None])
        along = jnp.einsum("qhd,khd->hqk", row_up, value_rows, preferred_element_type=jnp.float32)
        inner = jnp.sum(along * probs, axis=-1, keepdims=True)
        score_grad = (probs * (along - inner)).astype(jnp.bfloat16)
        query_grads.append(
            jnp.einsum("hqk,khd->qhd", score_grad, key_rows, preferred_element_type=jnp.float32)
            * score_scale
        )
        grad_keys = (
            grad_keys
            + jnp.einsum("hqk,qhd->khd", score_grad, row_query, preferred_element_type=jnp.float32)
            * score_scale
        )
        grad_values = grad_values + jnp.einsum(
            "hqk,qhd->khd", probs.astype(jnp.bfloat16), row_up, preferred_element_type=jnp.float32
        )
    return (jnp.concatenate(query_grads, 0), grad_keys, grad_values)


def on_device(
    residual_in,
    piece_ids,
    norm_gains,
    qkv_weight,
    qv_bias,
    out_weight,
    fc_weight,
    fc_bias,
    proj_weight,
    out_biases,
    cotangent,
):
    residual_rows, upstream_rows, labels_all = (residual_in, cotangent, piece_ids)
    qkv_w, qv_b, out_w, fc_w, fc_b, proj_w = (
        qkv_weight,
        qv_bias,
        out_weight,
        fc_weight,
        fc_bias,
        proj_weight,
    )
    seq_count, local_len, compact_width = residual_rows.shape
    local_rows = seq_count * local_len
    local_width = qkv_w.shape[2]
    head_count = local_width // HD
    gain_values = norm_gains.astype(jnp.float32)
    bias_values = qv_b.astype(jnp.float32)
    end_biases = out_biases.astype(jnp.float32)
    inputs_flat = residual_rows.reshape(local_rows, compact_width).astype(jnp.float32)
    normed_one, norm_one_back = jax.vjp(crms_gain, inputs_flat, gain_values[0])
    one_low = normed_one.astype(jnp.bfloat16).reshape(seq_count, local_len, D)
    full_one = lax.all_gather(one_low, "tensor", axis=1, tiled=True)
    seq_len = full_one.shape[1]
    token_count = seq_count * seq_len
    flat_one = full_one.reshape(token_count, D)
    projected = jnp.einsum("td,cde->cte", flat_one, qkv_w, preferred_element_type=jnp.float32)
    queries = (
        (projected[0] + bias_values[0])
        .astype(jnp.bfloat16)
        .reshape(seq_count, seq_len, head_count, HD)
    )
    key_rows = projected[1].astype(jnp.bfloat16).reshape(seq_count, seq_len, head_count, HD)
    value_rows = (
        (projected[2] + bias_values[1])
        .astype(jnp.bfloat16)
        .reshape(seq_count, seq_len, head_count, HD)
    )
    attended, log_sums = lax.map(attend_forward, (queries, key_rows, value_rows, labels_all))
    attended_flat = attended.reshape(token_count, local_width)
    branch_part = jnp.dot(attended_flat, out_w, preferred_element_type=jnp.float32).reshape(
        seq_count, seq_len, compact_width
    )
    branch_sum = lax.psum_scatter(
        branch_part.astype(jnp.bfloat16), "tensor", scatter_dimension=1, tiled=True
    ).astype(jnp.float32)
    middle = inputs_flat + branch_sum.reshape(local_rows, compact_width) + end_biases[0]
    normed_two, norm_two_back = jax.vjp(crms_gain, middle, gain_values[1])
    two_low = normed_two.astype(jnp.bfloat16).reshape(seq_count, local_len, D)
    full_two = lax.all_gather(two_low, "tensor", axis=1, tiled=True).reshape(token_count, D)
    hidden_pre = jnp.dot(full_two, fc_w, preferred_element_type=jnp.float32) + fc_b.astype(
        jnp.float32
    )
    active_full, gelu_back = jax.vjp(gelu_tanh, hidden_pre)
    active = active_full.astype(jnp.bfloat16)
    mlp_part = jnp.dot(active, proj_w, preferred_element_type=jnp.float32).reshape(
        seq_count, seq_len, compact_width
    )
    mlp_sum = lax.psum_scatter(
        mlp_part.astype(jnp.bfloat16), "tensor", scatter_dimension=1, tiled=True
    ).astype(jnp.float32)
    block_out = (
        (middle + mlp_sum.reshape(local_rows, compact_width) + end_biases[1])
        .astype(jnp.bfloat16)
        .reshape(seq_count, local_len, compact_width)
    )
    upstream_full = lax.all_gather(upstream_rows, "tensor", axis=1, tiled=True).reshape(
        token_count, compact_width
    )
    upstream_flat = upstream_rows.reshape(local_rows, compact_width).astype(jnp.float32)
    grad_proj_weight = jnp.dot(active.T, upstream_full, preferred_element_type=jnp.float32)
    hidden_grad = gelu_back(jnp.dot(upstream_full, proj_w.T, preferred_element_type=jnp.float32))[
        0
    ].astype(jnp.bfloat16)
    grad_fc_weight = jnp.dot(full_two.T, hidden_grad, preferred_element_type=jnp.float32)
    grad_fc_bias = jnp.sum(hidden_grad.astype(jnp.float32), axis=0)
    two_part = jnp.dot(hidden_grad, fc_w.T, preferred_element_type=jnp.float32).reshape(
        seq_count, seq_len, D
    )
    two_grad = (
        lax.psum_scatter(two_part.astype(jnp.bfloat16), "tensor", scatter_dimension=1, tiled=True)
        .astype(jnp.float32)
        .reshape(local_rows, D)
    )
    middle_norm_grad, gain_two_grad = norm_two_back(two_grad)
    middle_grad = upstream_flat + middle_norm_grad
    branch_low = middle_grad.astype(jnp.bfloat16)
    branch_seq = branch_low.reshape(seq_count, local_len, compact_width)
    branch_full = lax.all_gather(branch_seq, "tensor", axis=1, tiled=True).reshape(
        token_count, compact_width
    )
    grad_out_weight = jnp.dot(attended_flat.T, branch_full, preferred_element_type=jnp.float32)
    attended_grad = (
        jnp.dot(branch_full, out_w.T, preferred_element_type=jnp.float32)
        .astype(jnp.bfloat16)
        .reshape(seq_count, seq_len, head_count, HD)
    )
    query_grad, key_grad, value_grad = lax.map(
        attend_backward, (queries, key_rows, value_rows, labels_all, attended_grad, log_sums)
    )
    stacked = (
        jnp.stack([query_grad, key_grad, value_grad])
        .astype(jnp.bfloat16)
        .reshape(3, token_count, local_width)
    )
    grad_qkv = jnp.einsum("td,cte->cde", flat_one, stacked, preferred_element_type=jnp.float32)
    grad_qv_bias = jnp.stack(
        [
            jnp.sum(stacked[0].astype(jnp.float32), axis=0),
            jnp.sum(stacked[2].astype(jnp.float32), axis=0),
        ]
    )
    one_part = jnp.einsum(
        "cte,cde->td", stacked, qkv_w, preferred_element_type=jnp.float32
    ).reshape(seq_count, seq_len, D)
    one_grad = (
        lax.psum_scatter(one_part.astype(jnp.bfloat16), "tensor", scatter_dimension=1, tiled=True)
        .astype(jnp.float32)
        .reshape(local_rows, D)
    )
    input_norm_grad, gain_one_grad = norm_one_back(one_grad)
    grad_input = (
        (middle_grad + input_norm_grad)
        .astype(jnp.bfloat16)
        .reshape(seq_count, local_len, compact_width)
    )
    gain_terms = jnp.stack([gain_one_grad, gain_two_grad])
    bias_terms = jnp.stack(
        [jnp.sum(branch_low.astype(jnp.float32), axis=0), jnp.sum(upstream_flat, axis=0)]
    )
    grad_gains, grad_out_biases = lax.psum((gain_terms, bias_terms), ("dp", "group", "tensor"))
    weight_grads = (
        grad_qkv,
        grad_qv_bias,
        grad_out_weight,
        grad_fc_weight,
        grad_fc_bias,
        grad_proj_weight,
    )
    shards = (
        lax.psum_scatter(
            weight_grads[0].astype(jnp.bfloat16), "dp", scatter_dimension=1, tiled=True
        ).astype(jnp.float32),
        lax.psum_scatter(
            weight_grads[1].astype(jnp.bfloat16), "dp", scatter_dimension=1, tiled=True
        ).astype(jnp.float32),
        lax.psum_scatter(
            weight_grads[2].astype(jnp.bfloat16), "dp", scatter_dimension=0, tiled=True
        ).astype(jnp.float32),
        lax.psum_scatter(
            weight_grads[3].astype(jnp.bfloat16), "dp", scatter_dimension=0, tiled=True
        ).astype(jnp.float32),
        lax.psum_scatter(
            weight_grads[4].astype(jnp.bfloat16), "dp", scatter_dimension=0, tiled=True
        ).astype(jnp.float32),
        lax.psum_scatter(
            weight_grads[5].astype(jnp.bfloat16), "dp", scatter_dimension=0, tiled=True
        ).astype(jnp.float32),
    )
    reduced = (
        lax.psum(shards[0].astype(jnp.bfloat16), "group").astype(jnp.float32),
        lax.psum(shards[1].astype(jnp.bfloat16), "group").astype(jnp.float32),
        lax.psum(shards[2].astype(jnp.bfloat16), "group").astype(jnp.float32),
        lax.psum(shards[3].astype(jnp.bfloat16), "group").astype(jnp.float32),
        lax.psum(shards[4].astype(jnp.bfloat16), "group").astype(jnp.float32),
        lax.psum(shards[5].astype(jnp.bfloat16), "group").astype(jnp.float32),
    )
    return (
        block_out,
        grad_input,
        grad_gains,
        reduced[0],
        reduced[1],
        reduced[2],
        reduced[3],
        reduced[4],
        reduced[5],
        grad_out_biases,
    )


def solution(mesh):
    in_specs = (
        P(("dp", "group"), "tensor", None),
        P(("dp", "group"), None),
        P(),
        P(None, None, "tensor"),
        P(None, "tensor"),
        P("tensor", None),
        P(None, "tensor"),
        P("tensor"),
        P("tensor", None),
        P(),
        P(("dp", "group"), "tensor", None),
    )
    out_specs = (
        P(("dp", "group"), "tensor", None),
        P(("dp", "group"), "tensor", None),
        P(),
        P(None, "dp", "tensor"),
        P(None, ("tensor", "dp")),
        P(("tensor", "dp"), None),
        P("dp", "tensor"),
        P(("tensor", "dp")),
        P(("tensor", "dp"), None),
        P(),
    )
    return jax.shard_map(
        on_device, mesh=mesh, in_specs=in_specs, out_specs=out_specs, check_vma=False
    )
```

profile of v0, /device:TPU:0, one launch (start us, length us, event | category | flops | bytes accessed | tf_op | source)
XLA Modules:
  0.0 1026.2 jit_solution(11230917446306738538)
XLA Ops:
  7.2 5.2 copy.65
  18.4 3.7 copy.67
  28.7 47.5 %all-gather.5.cloned.1.call-done = bf16[2,1024,768]{2,1,0:T(8,128)(2,1)} async-done(((bf16[2,512,768]{2,1,0:T(8,128)(2,1)}), bf16[2,1024,768]{2,1,0:T(8,128)(2,1)}) %all-gather.5.cloned.1.call-update) | async-done | bytes 3145744 | tf_op jit(solution)/shard_map/all_gather | solution.py:128
  76.2 6.8 convolution_bitcast_fusion
  90.9 5.6 squeeze.35
  103.8 3.9 convert_element_type.203
  114.3 5.6 squeeze.34
  124.6 54.4 %while.26 = (s32[]{:T(128)}, bf16[2,1024,6,64]{1,3,2,0:T(8,128)(2,1)}, f32[2,6,1024]{2,1,0:T(8,128)}, bf16[2,1024,6,64]{1,3,2,0:T(8,128)(2,1)}, s32[2,1024]{1,0:...) while((s32[]{:T(128)}, ...), condition=%wide.region_7.8_spmd, body=%wide.region_2.7_spmd.sunk | while | flops 1692272128 | bytes 111457016 | solution.py:144
  127.7 3.6 fusion.157
  131.3 3.6 fusion.158
  135.0 3.9 fusion.159
  146.0 3.9 fusion.162
  154.7 3.6 fusion.157
  162.0 3.9 fusion.159
  173.0 3.9 fusion.162
  179.0 4.8 convolution_convert_fusion.5
  185.3 42.1 %reduce-scatter.14.cloned.1.call-done = bf16[2,512,767]{2,1,0:T(8,128)(2,1)} async-done(((bf16[2,1024,767]{2,1,0:T(8,128)(2,1)}), bf16[2,512,767]{2,1,0:T(8,128)(2,1)}) %reduce-scatter.14.cloned.1.call-update) | async-done | bytes 1570832 | tf_op jit(solution)/shard_map/reduce_scatter | solution.py:149
  227.4 4.0 fusion.94
  234.9 3.9 add_add_fusion.2
  244.4 29.4 %all-gather.9.cloned.1.call-done = bf16[2,1024,767]{1,0,2:T(2,128)(2,1)} async-done(((bf16[2,512,767]{1,0,2:T(2,128)(2,1)}), bf16[2,1024,767]{1,0,2:T(2,128)(2,1)}) %all-gather.9.cloned.1.call-update) | async-done | bytes 3141648 | tf_op jit(solution)/shard_map/all_gather | solution.py:172
  273.9 4.3 pad.21
  280.9 39.4 %all-gather.7.cloned.1.call-done = bf16[2,1024,768]{2,1,0:T(8,128)(2,1)} async-done(((bf16[2,512,768]{2,1,0:T(8,128)(2,1)}), bf16[2,1024,768]{2,1,0:T(8,128)(2,1)}) %all-gather.7.cloned.1.call-update) | async-done | bytes 3145744 | tf_op jit(solution)/shard_map/all_gather | solution.py:155
  320.3 13.8 %multiply_convert_fusion.2 = (bf16[2048,1536]{1,0:T(8,128)(2,1)}, f32[2048,1536]{1,0:T(8,128)}) fusion(f32[1536]{0:T(1024)S(1)} %convert_element_type.208, bf16[2048,768]{1,0:T(8,128)(2,1)} %bitcast.353, bf16[768,1536]{1,0:T(8,128)(2,1)S(1)} %copy-done), kind=kOutput, calls=%fused_computation.125 | convolution fusion | flops 4863295488 | bytes 24385536 | tf_op jit(solution)/shard_map/dot_general | solution.py:156
  334.1 15.3 %fusion.97 = (bf16[1536]{0:T(1024)(128)(2,1)}, bf16[2048,1536]{1,0:T(8,128)(2,1)S(1)}) fusion(f32[2048,1536]{1,0:T(8,128)} %get-tuple-element.273, f32[1536]{0:T(1024)S(1)} %convert_element_type.208, bf16[2048,767]{0,1:T(8,128)(2,1)S(1)} %bitcast.318, bf16[1536,767]{1,0:T(8,128)(2,1)S(1)} %copy-done.63), kind=kOutput, calls=%fused_computation.195 | convolution fusion | flops 4894751232 | bytes 24381440 | tf_op jit(solution)/shard_map/dot_general | solution.py:177
  349.4 6.4 convolution_convert_fusion.2
  362.0 37.4 %reduce-scatter.18.cloned.1.call-done = bf16[2,512,768]{2,1,0:T(8,128)(2,1)} async-done(((bf16[2,1024,768]{2,1,0:T(8,128)(2,1)}), bf16[2,512,768]{2,1,0:T(8,128)(2,1)}) %reduce-scatter.18.cloned.1.call-update) | async-done | bytes 1572880 | tf_op jit(solution)/shard_map/reduce_scatter | solution.py:186
  412.4 44.9 %all-gather.11.cloned.1.call-done = bf16[2,1024,767]{1,0,2:T(2,128)(2,1)} async-done(((bf16[2,512,767]{1,0,2:T(2,128)(2,1)}), bf16[2,1024,767]{1,0,2:T(2,128)(2,1)}) %all-gather.11.cloned.1.call-update) | async-done | bytes 3141648 | tf_op jit(solution)/shard_map/all_gather | solution.py:194
  457.3 4.3 pad.22
  472.5 133.8 %while.27 = (s32[]{:T(128)}, bf16[2,1024,6,64]{1,3,2,0:T(8,128)(2,1)}, bf16[2,1024,6,64]{1,3,2,0:T(8,128)(2,1)}, bf16[2,1024,6,64]{1,3,2,0:T(8,128)(2,1)}, bf16[...) while((s32[]{:T(128)}, ...), condition=%wide.region_17.18_spmd, body=%wide.region_14.17_spmd.sunk | while | flops 4128632320 | bytes 286275584 | solution.py:203
  482.8 4.4 fusion.183
  487.3 5.5 bitcast_dynamic-update-slice_fusion.5
  492.8 8.4 multiply_reduce_fusion.10
  501.2 9.6 multiply_convert_fusion.7
  510.8 5.2 fusion.178
  516.0 8.1 multiply_reduce_fusion.11
  524.1 7.0 multiply_convert_fusion.8
  549.5 4.4 fusion.183
  553.9 5.5 bitcast_dynamic-update-slice_fusion.5
  559.4 8.4 multiply_reduce_fusion.10
  567.8 9.6 multiply_convert_fusion.7
  577.5 5.2 fusion.178
  582.7 8.1 multiply_reduce_fusion.11
  590.8 7.0 multiply_convert_fusion.8
  614.7 3.8 stack.48
  628.0 4.9 convert_bitcast_fusion.1
  632.9 4.0 copy.94
  638.5 9.4 convolution_convert_fusion
  648.0 9.4 convolution_convert_fusion.1
  663.5 9.0 convolution_convert_fusion.3
  678.5 25.3 %reduce-scatter.26.cloned.1.call-done = bf16[384,767]{1,0:T(8,128)(2,1)} async-done(((bf16[1536,767]{1,0:T(8,128)(2,1)}), bf16[384,767]{1,0:T(8,128)(2,1)}) %reduce-scatter.26.cloned.1.call-update) | async-done | bytes 589072 | tf_op jit(solution)/shard_map/reduce_scatter | solution.py:261
  703.8 35.6 %reduce-scatter.24.cloned.1.call-done = bf16[192,1536]{1,0:T(8,128)(2,1)} async-done(((bf16[768,1536]{1,0:T(8,128)(2,1)}), bf16[192,1536]{1,0:T(8,128)(2,1)}) %reduce-scatter.24.cloned.1.call-update) | async-done | bytes 589840 | tf_op jit(solution)/shard_map/reduce_scatter | solution.py:255
  739.4 25.2 %reduce-scatter.22.cloned.1.call-done = bf16[96,767]{1,0:T(8,128)(2,1)} async-done(((bf16[384,767]{1,0:T(8,128)(2,1)}), bf16[96,767]{1,0:T(8,128)(2,1)}) %reduce-scatter.22.cloned.1.call-update) | async-done | bytes 147280 | tf_op jit(solution)/shard_map/reduce_scatter | solution.py:252
  764.7 7.0 copy.87
  771.7 9.1 bitcast_convert_fusion
  780.8 3.7 convert_reduce_fusion
  785.8 6.1 all-reduce
  792.0 18.4 %reduce-scatter.16.cloned.1.call-done = bf16[2,512,767]{2,1,0:T(8,128)(2,1)} async-done(((bf16[2,1024,767]{2,1,0:T(8,128)(2,1)}), bf16[2,512,767]{2,1,0:T(8,128)(2,1)}) %reduce-scatter.16.cloned.1.call-update) | async-done | bytes 1570832 | tf_op jit(solution)/shard_map/reduce_scatter | solution.py:164
  813.3 4.9 copy.90
  818.3 14.5 %reduce-scatter.30.cloned.1.call-done = bf16[96,2]{1,0:T(8,128)(2,1)} async-done(((bf16[384,2]{1,0:T(8,128)(2,1)}), bf16[96,2]{1,0:T(8,128)(2,1)}) %reduce-scatter.30.cloned.1.call-update) | async-done | bytes 400
  833.6 11.8 %all-reduce.2 = (bf16[2,96]{1,0:T(2,128)(2,1)S(1)}, bf16[384]{0:T(512)(128)(2,1)S(1)}) all-reduce(bf16[2,96]{1,0:T(2,128)(2,1)S(1)} %copy.97, bf16[384]{0:T(512)(128)(2,1)S(1)} %dynamic-slice.1), channel_id=1, replica_groups=mesh['dp'=4,'group'=4,'tensor'=2] {'group'}, use_global_device_ids=true, to_apply=%region_28.29 | all-reduce | flops 576 | bytes 2304 | tf_op jit(solution)/shard_map/psum | solution.py:267
  846.5 71.2 %all-reduce.6.cloned.1.call-done = (bf16[3,192,384]{1,2,0:T(8,128)(2,1)}, bf16[96,767]{1,0:T(8,128)(2,1)}, bf16[192,1536]{1,0:T(8,128)(2,1)}, bf16[384,767]{1,0:T(8,128)(2,1)}) async-done(((bf16[3,192,384]{1,2,0:T(8,128)(2,1)}, bf16[96,767]{1,0:T(8,128)(2,1)}, bf16[192,1536]{1,0:T(8,128)(2,1)}, bf16[384,767]{1,0:T(8,128)(2,1)}), (bf16[3,192,384]{1,2,0:T(8,128)(2,1)}, bf16[96,767]{1,0:T(8,128)(2,1)}, ...) | async-done | bytes 1768528 | tf_op jit(solution)/shard_map/psum | solution.py:266
  926.1 36.2 %reduce-scatter.20.cloned.1.call-done = bf16[2,512,768]{2,1,0:T(8,128)(2,1)} async-done(((bf16[2,1024,768]{2,1,0:T(8,128)(2,1)}), bf16[2,512,768]{2,1,0:T(8,128)(2,1)}) %reduce-scatter.20.cloned.1.call-update) | async-done | bytes 1572880 | tf_op jit(solution)/shard_map/reduce_scatter | solution.py:222
  974.5 5.2 reshape.591
  979.7 39.6 %all-reduce.1 = (f32[2,768]{1,0:T(2,128)}, f32[2,767]{1,0:T(2,128)}) all-reduce(f32[2,768]{1,0:T(2,128)S(1)} %pad_maximum_fusion.4, f32[2,767]{1,0:T(2,128)S(1)} %pad_maximum_fusion.5), channel_id=1, replica_groups=mesh['dp'=4,'group'=4,'tensor'=2] {'dp','group','tensor'}, use_global_device_ids=true, to_apply=%region_22.23 | all-reduce | flops 3070 | bytes 24560 | tf_op jit(solution)/shard_map/psum | solution.py:236
  (355 shorter events, 203.5 us)
Async XLA Ops:
  7.2 313.1 %copy-start = (bf16[768,1536]{1,0:T(8,128)(2,1)S(1)}, bf16[768,1536]{1,0:T(8,128)(2,1)}, u32[]{:S(2)}) copy-start(bf16[768,1536]{1,0:T(8,128)(2,1)} %param.21) | copy-start | bytes 7077892
  7.2 69.0 %all-gather.5.cloned.1.call-start = ((), (), s32[]{:S(2)}) async-start(), calls=%async_computation.9 | async-start | bytes 4718592 | tf_op jit(solution)/shard_map/all_gather | solution.py:128
  12.4 5.1 copy-start.58
  18.1 6.7 copy-start.40
  18.1 3.9 copy-start.43
  18.3 6.5 copy-start.31
  24.8 3.6 copy-start.51
  24.8 3.5 copy-start.45
  24.9 3.6 copy-start.60
  28.4 199.0 %reduce-scatter.14.cloned.1.call-start = ((), (), s32[]{:S(2)}) async-start(), calls=%async_computation.10 | async-start | bytes 4718592 | tf_op jit(solution)/shard_map/reduce_scatter | solution.py:149
  124.6 54.4 %copy-start.65 = (bf16[384,767]{1,0:T(8,128)(2,1)S(1)}, bf16[384,767]{1,0:T(8,128)(2,1)}, u32[]{:S(2)}) copy-start(bf16[384,767]{1,0:T(8,128)(2,1)} %param.20) | copy-start | bytes 1767172
  131.3 3.7 copy-start.8
  135.0 3.9 copy-start.2
  146.0 4.5 copy-start.36
  158.3 3.7 copy-start.8
  162.0 3.9 copy-start.2
  173.0 4.5 copy-start.36
  183.9 90.0 %all-gather.9.cloned.1.call-start = ((), (), s32[]{:S(2)}) async-start(), calls=%async_computation.13 | async-start | bytes 4712448 | tf_op jit(solution)/shard_map/all_gather | solution.py:172
  184.6 135.7 %all-gather.7.cloned.1.call-start = ((), (), s32[]{:S(2)}) async-start(), calls=%async_computation.11 | async-start | bytes 4718592 | tf_op jit(solution)/shard_map/all_gather | solution.py:155
  231.6 9.2 copy-start.32
  240.8 3.6 copy-start.56
  244.4 155.0 %reduce-scatter.18.cloned.1.call-start = ((), (), s32[]{:S(2)}) async-start(), calls=%async_computation.14 | async-start | bytes 4718592 | tf_op jit(solution)/shard_map/reduce_scatter | solution.py:186
  320.3 13.8 %copy-start.33 = (bf16[96,8,2,1024]{3,1,2,0:T(8,128)(2,1)S(1)}, bf16[96,8,2,1024]{3,1,2,0:T(8,128)(2,1)}, u32[]{:S(2)}) copy-start(bf16[96,8,2,1024]{3,1,2,0:T(8,128)(2,1)} %copy.101) | copy-start | bytes 9437188
  320.3 13.8 %copy-start.63 = (bf16[1536,767]{1,0:T(8,128)(2,1)S(1)}, bf16[1536,767]{1,0:T(8,128)(2,1)}, u32[]{:S(2)}) copy-start(bf16[1536,767]{1,0:T(8,128)(2,1)} %param.23) | copy-start | bytes 7068676
  349.4 6.4 copy-start.68
  355.9 101.4 %all-gather.11.cloned.1.call-start = ((), (), s32[]{:S(2)}) async-start(), calls=%async_computation.15 | async-start | bytes 4712448 | tf_op jit(solution)/shard_map/all_gather | solution.py:194
  359.5 39.9 %copy-start.11 = (f32[2,512,767]{2,1,0:T(8,128)S(1)}, f32[2,512,767]{2,1,0:T(8,128)}, u32[]{:S(2)}) copy-start(f32[2,512,767]{2,1,0:T(8,128)} %get-tuple-element.243) | copy-start | bytes 9424900
  412.3 263.4 %reduce-scatter.28.cloned.1.call-start = ((), (), s32[]{:S(2)}) async-start(), calls=%async_computation.20 | async-start | bytes 2211840
  467.0 5.5 copy-start.3
  476.6 10.7 %copy-start.5 = (pred[512,1024]{1,0:T(8,128)(4,1)}, pred[512,1024]{1,0:T(8,128)(4,1)S(1)}, u32[]{:S(2)}) copy-start(pred[512,1024]{1,0:T(8,128)(4,1)S(1)} %get-tuple-element.421) | copy-start | bytes 1572868 | tf_op jit(solution)/shard_map/while
  510.8 5.2 copy-start.6
  510.8 5.2 copy-start.9
  524.1 7.0 copy-start.4
  543.2 10.7 %copy-start.5 = (pred[512,1024]{1,0:T(8,128)(4,1)}, pred[512,1024]{1,0:T(8,128)(4,1)S(1)}, u32[]{:S(2)}) copy-start(pred[512,1024]{1,0:T(8,128)(4,1)S(1)} %get-tuple-element.421) | copy-start | bytes 1572868 | tf_op jit(solution)/shard_map/while
  577.4 5.2 copy-start.6
  577.4 5.2 copy-start.9
  590.8 7.0 copy-start.4
  606.3 5.6 copy-start.23
  611.9 6.6 copy-start.27
  624.4 3.5 copy-start.61
  638.5 65.3 %reduce-scatter.26.cloned.1.call-start = ((), (), s32[]{:S(2)}) async-start(), calls=%async_computation.19 | async-start | bytes 2949120 | tf_op jit(solution)/shard_map/reduce_scatter | solution.py:261
  638.5 9.4 copy-start.62
  647.9 91.5 %reduce-scatter.24.cloned.1.call-start = ((), (), s32[]{:S(2)}) async-start(), calls=%async_computation.18 | async-start | bytes 2949120 | tf_op jit(solution)/shard_map/reduce_scatter | solution.py:255
  657.4 3.7 copy-start.35
  657.4 107.2 %reduce-scatter.22.cloned.1.call-start = ((), (), s32[]{:S(2)}) async-start(), calls=%async_computation.17 | async-start | bytes 737280 | tf_op jit(solution)/shard_map/reduce_scatter | solution.py:252
  663.4 146.9 %reduce-scatter.16.cloned.1.call-start = ((), (), s32[]{:S(2)}) async-start(), calls=%async_computation.12 | async-start | bytes 4718592 | tf_op jit(solution)/shard_map/reduce_scatter | solution.py:164
  672.5 160.2 %reduce-scatter.30.cloned.1.call-start = ((), (), s32[]{:S(2)}) async-start(), calls=%async_computation.21 | async-start | bytes 122880
  675.7 242.0 %all-reduce.6.cloned.1.call-start = ((), (), s32[]{:S(2)}) async-start(), calls=%async_computation.22 | async-start | bytes 3833856 | tf_op jit(solution)/shard_map/psum | solution.py:266
  764.6 197.6 %reduce-scatter.20.cloned.1.call-start = ((), (), s32[]{:S(2)}) async-start(), calls=%async_computation.16 | async-start | bytes 4718592 | tf_op jit(solution)/shard_map/reduce_scatter | solution.py:222
  764.7 7.1 copy-start.64
  780.8 3.7 copy-start.67
  780.8 5.0 copy-start.57
  780.8 29.5 %copy-start.12 = (f32[2,512,767]{2,1,0:T(8,128)S(1)}, f32[2,512,767]{2,1,0:T(8,128)}, u32[]{:S(2)}) copy-start(f32[2,512,767]{2,1,0:T(8,128)} %get-tuple-element.243) | copy-start | bytes 9424900
  780.8 29.5 %copy-start.55 = (f32[767]{0:T(1024)S(1)}, f32[767]{0:T(1024)}, u32[]{:S(2)}) copy-start(f32[767]{0:T(1024)} %get-tuple-element.192) | copy-start | bytes 9208
  813.3 4.9 copy-start.53
  813.3 4.9 copy-start.54
  818.2 144.0 %copy-start.10 = (f32[2,512,767]{2,1,0:T(8,128)S(1)}, f32[2,512,767]{2,1,0:T(8,128)}, u32[]{:S(2)}) copy-start(f32[2,512,767]{2,1,0:T(8,128)} %convert_element_type.195) | copy-start | bytes 9424900
  818.2 144.0 %copy-start.41 = (f32[768]{0:T(1024)S(1)}, f32[768]{0:T(1024)}, u32[]{:S(2)}) copy-start(f32[768]{0:T(1024)} %copy-done.40) | copy-start | bytes 9220
  818.2 144.0 %copy-start.46 = (f32[2,512]{1,0:T(2,128)S(1)}, f32[2,512]{1,0:T(2,128)}, u32[]{:S(2)}) copy-start(f32[2,512]{1,0:T(2,128)} %copy-done.45) | copy-start | bytes 12292
  923.8 41.2 %copy-start.50 = (f32[1024]{0:T(1024)S(1)}, f32[1024]{0:T(1024)}, u32[]{:S(2)}) copy-start(f32[1024]{0:T(1024)} %copy-done.49) | copy-start | bytes 12292
  964.9 3.3 copy-start.13
  968.3 3.8 copy-start.17
  968.3 3.8 copy-start.48
  972.1 47.2 %copy-start.1 = (bf16[768,1536]{1,0:T(8,128)(2,1)S(1)}, bf16[768,1536]{1,0:T(8,128)(2,1)}, u32[]{:S(2)}) copy-start(bf16[768,1536]{1,0:T(8,128)(2,1)} %param.21) | copy-start | bytes 7077892
  (37 other events, 76.3 us)
Sparse Core Ops, SparseCore 0:
  28.5 47.6 all-gather.4
  184.0 43.3 reduce-scatter.13
  229.0 44.8 all-gather.8
  275.3 44.9 all-gather.6
  356.0 43.3 reduce-scatter.17
  412.4 44.8 all-gather.10
  638.6 29.3 reduce-scatter.27
  670.7 33.0 reduce-scatter.25
  706.3 33.0 reduce-scatter.23
  742.5 22.0 reduce-scatter.21
  766.9 43.3 reduce-scatter.15
  813.2 19.5 reduce-scatter.29
  836.0 81.7 all-reduce.5
  919.8 42.3 reduce-scatter.19
where the time goes:
time: 1040 us; the launch traced here: 1030 us
  waiting for transfers between devices  468 us (45%)
  matrix products  207 us (20%)
  local copies, waits for them, and re-layouts  161 us (15%)
  other arithmetic  114 us (11%)
  blocking collectives  57.5 us (6%)
  between operations  15.8 us (2%)
    psum x1, waiting for transfers between devices, on_device(): lax.psum(shards[0].astype(jnp.bfloat16), 'group').astype(jnp.float32)  71.2 us
    unnamed x134, local copies, waits for them, and re-layouts  50.8 us
    all_gather x1, waiting for transfers between devices, on_device(): full_one = lax.all_gather(one_low, 'tensor', axis=1, tiled=True)  47.5 us
    all_gather x1, waiting for transfers between devices, on_device(): lax.all_gather(branch_seq, 'tensor', axis=1, tiled=True)  44.9 us
    reduce_scatter x1, waiting for transfers between devices, on_device(): lax.psum_scatter(branch_part.astype(jnp.bfloat16), 'tensor', scatter_dime...  42.1 us
    psum x1, blocking collectives, on_device(): lax.psum((gain_terms, bias_terms), ('dp', 'group', 'tensor'))  39.6 us
    all_gather x1, waiting for transfers between devices, on_device(): lax.all_gather(two_low, 'tensor', axis=1, tiled=True)  39.4 us
    reduce_scatter x1, waiting for transfers between devices, on_device(): lax.psum_scatter(two_part.astype(jnp.bfloat16), 'tensor', scatter_dimensi...  37.4 us
  transfers between devices with their start and end apart: 14, of which 13 were waited for; matrix products, arithmetic and copies ran while one was open for 10% of the time, Pallas kernels for 0%

commit v1 on v0

--- a/solution.py
+++ b/solution.py
@@ -7,6 +7,11 @@
 HD = 64
 EPSILON = 1e-05
 MASKED = -1e30
+
+
+def by_each_axis(x, first, second):
+    half = lax.psum(x, first)
+    return lax.psum(half, second)
 
 
 def decompress(compact):
@@ -233,7 +238,7 @@
     bias_terms = jnp.stack(
         [jnp.sum(branch_low.astype(jnp.float32), axis=0), jnp.sum(upstream_flat, axis=0)]
     )
-    grad_gains, grad_out_biases = lax.psum((gain_terms, bias_terms), ("dp", "group", "tensor"))
+    grad_gains, grad_out_biases = by_each_axis((gain_terms, bias_terms), ("group", "tensor"), "dp")
     weight_grads = (
         grad_qkv,
         grad_qv_bias,

time: 1040 us -> 1050 us (level)
    psum x1 -> x2, blocking collectives: 39.6 us -> 46.9 us  [the longest x1 36.1 us: by_each_axis(): half = lax.psum(x, first)]
where the time goes in v1:
time: 1050 us; the launch traced here: 1030 us
  waiting for transfers between devices  468 us (45%)
  matrix products  208 us (20%)
  local copies, waits for them, and re-layouts  161 us (15%)
  other arithmetic  114 us (11%)
  blocking collectives  64.8 us (6%)
  between operations  15.8 us (2%)
    psum x1, waiting for transfers between devices, on_device(): lax.psum(shards[0].astype(jnp.bfloat16), 'group').astype(jnp.float32)  71.2 us
    unnamed x134, local copies, waits for them, and re-layouts  50.8 us
    all_gather x1, waiting for transfers between devices, on_device(): full_one = lax.all_gather(one_low, 'tensor', axis=1, tiled=True)  47.5 us
    all_gather x1, waiting for transfers between devices, on_device(): lax.all_gather(branch_seq, 'tensor', axis=1, tiled=True)  44.9 us
    reduce_scatter x1, waiting for transfers between devices, on_device(): lax.psum_scatter(branch_part.astype(jnp.bfloat16), 'tensor', scatter_dime...  42.1 us
    all_gather x1, waiting for transfers between devices, on_device(): lax.all_gather(two_low, 'tensor', axis=1, tiled=True)  39.4 us
    reduce_scatter x1, waiting for transfers between devices, on_device(): lax.psum_scatter(two_part.astype(jnp.bfloat16), 'tensor', scatter_dimensi...  37.4 us
    reduce_scatter x1, waiting for transfers between devices, on_device(): lax.psum_scatter(one_part.astype(jnp.bfloat16), 'tensor', scatter_dimensi...  36.2 us
  transfers between devices with their start and end apart: 14, of which 13 were waited for; matrix products, arithmetic and copies ran while one was open for 10% of the time, Pallas kernels for 0%

profile of v1, /device:TPU:0, one launch (start us, length us, event | category | flops | bytes accessed | tf_op | source)
XLA Modules:
  0.0 1033.7 jit_solution(865305445205281709)
XLA Ops:
  7.2 5.2 copy.65
  18.4 3.7 copy.67
  28.7 47.5 %all-gather.5.cloned.1.call-done = bf16[2,1024,768]{2,1,0:T(8,128)(2,1)} async-done(((bf16[2,512,768]{2,1,0:T(8,128)(2,1)}), bf16[2,1024,768]{2,1,0:T(8,128)(2,1)}) %all-gather.5.cloned.1.call-update) | async-done | bytes 3145744 | tf_op jit(solution)/shard_map/all_gather | solution.py:133
  76.2 6.8 convolution_bitcast_fusion
  91.0 5.6 squeeze.35
  103.9 3.8 convert_element_type.203
  114.3 5.6 squeeze.34
  124.7 54.3 %while.26 = (s32[]{:T(128)}, bf16[2,1024,6,64]{1,3,2,0:T(8,128)(2,1)}, f32[2,6,1024]{2,1,0:T(8,128)}, bf16[2,1024,6,64]{1,3,2,0:T(8,128)(2,1)}, s32[2,1024]{1,0:...) while((s32[]{:T(128)}, ...), condition=%wide.region_7.8_spmd, body=%wide.region_2.7_spmd.sunk | while | flops 1692272128 | bytes 111457016 | solution.py:149
  127.8 3.6 fusion.157
  135.1 3.9 fusion.159
  146.1 3.9 fusion.162
  154.8 3.6 fusion.157
  162.1 3.9 fusion.159
  173.1 3.9 fusion.162
  179.0 4.9 convolution_convert_fusion.5
  185.3 42.1 %reduce-scatter.14.cloned.1.call-done = bf16[2,512,767]{2,1,0:T(8,128)(2,1)} async-done(((bf16[2,1024,767]{2,1,0:T(8,128)(2,1)}), bf16[2,512,767]{2,1,0:T(8,128)(2,1)}) %reduce-scatter.14.cloned.1.call-update) | async-done | bytes 1570832 | tf_op jit(solution)/shard_map/reduce_scatter | solution.py:154
  227.4 4.0 fusion.94
  235.0 3.9 add_add_fusion.2
  244.5 29.4 %all-gather.9.cloned.1.call-done = bf16[2,1024,767]{1,0,2:T(2,128)(2,1)} async-done(((bf16[2,512,767]{1,0,2:T(2,128)(2,1)}), bf16[2,1024,767]{1,0,2:T(2,128)(2,1)}) %all-gather.9.cloned.1.call-update) | async-done | bytes 3141648 | tf_op jit(solution)/shard_map/all_gather | solution.py:177
  273.9 4.3 pad.21
  280.9 39.4 %all-gather.7.cloned.1.call-done = bf16[2,1024,768]{2,1,0:T(8,128)(2,1)} async-done(((bf16[2,512,768]{2,1,0:T(8,128)(2,1)}), bf16[2,1024,768]{2,1,0:T(8,128)(2,1)}) %all-gather.7.cloned.1.call-update) | async-done | bytes 3145744 | tf_op jit(solution)/shard_map/all_gather | solution.py:160
  320.4 13.9 %multiply_convert_fusion.2 = (bf16[2048,1536]{1,0:T(8,128)(2,1)}, f32[2048,1536]{1,0:T(8,128)}) fusion(f32[1536]{0:T(1024)S(1)} %convert_element_type.208, bf16[2048,768]{1,0:T(8,128)(2,1)} %bitcast.353, bf16[768,1536]{1,0:T(8,128)(2,1)S(1)} %copy-done), kind=kOutput, calls=%fused_computation.125 | convolution fusion | flops 4863295488 | bytes 24385536 | tf_op jit(solution)/shard_map/dot_general | solution.py:161
  334.3 15.3 %fusion.97 = (bf16[1536]{0:T(1024)(128)(2,1)}, bf16[2048,1536]{1,0:T(8,128)(2,1)S(1)}) fusion(f32[2048,1536]{1,0:T(8,128)} %get-tuple-element.275, f32[1536]{0:T(1024)S(1)} %convert_element_type.208, bf16[2048,767]{0,1:T(8,128)(2,1)S(1)} %bitcast.318, bf16[1536,767]{1,0:T(8,128)(2,1)S(1)} %copy-done.63), kind=kOutput, calls=%fused_computation.195 | convolution fusion | flops 4894751232 | bytes 24381440 | tf_op jit(solution)/shard_map/dot_general | solution.py:182
  349.6 6.4 convolution_convert_fusion.2
  362.1 37.4 %reduce-scatter.18.cloned.1.call-done = bf16[2,512,768]{2,1,0:T(8,128)(2,1)} async-done(((bf16[2,1024,768]{2,1,0:T(8,128)(2,1)}), bf16[2,512,768]{2,1,0:T(8,128)(2,1)}) %reduce-scatter.18.cloned.1.call-update) | async-done | bytes 1572880 | tf_op jit(solution)/shard_map/reduce_scatter | solution.py:191
  412.6 44.9 %all-gather.11.cloned.1.call-done = bf16[2,1024,767]{1,0,2:T(2,128)(2,1)} async-done(((bf16[2,512,767]{1,0,2:T(2,128)(2,1)}), bf16[2,1024,767]{1,0,2:T(2,128)(2,1)}) %all-gather.11.cloned.1.call-update) | async-done | bytes 3141648 | tf_op jit(solution)/shard_map/all_gather | solution.py:199
  457.5 4.3 pad.22
  472.6 133.9 %while.27 = (s32[]{:T(128)}, bf16[2,1024,6,64]{1,3,2,0:T(8,128)(2,1)}, bf16[2,1024,6,64]{1,3,2,0:T(8,128)(2,1)}, bf16[2,1024,6,64]{1,3,2,0:T(8,128)(2,1)}, bf16[...) while((s32[]{:T(128)}, ...), condition=%wide.region_17.18_spmd, body=%wide.region_14.17_spmd.sunk | while | flops 4128632320 | bytes 286275584 | solution.py:208
  483.0 4.4 fusion.183
  487.4 5.5 bitcast_dynamic-update-slice_fusion.5
  492.9 8.5 multiply_reduce_fusion.10
  501.4 9.6 multiply_convert_fusion.7
  511.0 5.2 fusion.178
  516.2 8.1 multiply_reduce_fusion.11
  524.3 7.0 multiply_convert_fusion.8
  549.6 4.4 fusion.183
  554.1 5.5 bitcast_dynamic-update-slice_fusion.5
  559.6 8.4 multiply_reduce_fusion.10
  568.0 9.6 multiply_convert_fusion.7
  577.6 5.2 fusion.178
  582.8 8.1 multiply_reduce_fusion.11
  591.0 7.0 multiply_convert_fusion.8
  614.9 3.8 stack.48
  628.2 4.9 convert_bitcast_fusion.1
  633.1 4.0 copy.94
  638.7 9.3 convolution_convert_fusion
  648.2 9.4 convolution_convert_fusion.1
  663.6 9.0 convolution_convert_fusion.3
  678.7 25.3 %reduce-scatter.26.cloned.1.call-done = bf16[384,767]{1,0:T(8,128)(2,1)} async-done(((bf16[1536,767]{1,0:T(8,128)(2,1)}), bf16[384,767]{1,0:T(8,128)(2,1)}) %reduce-scatter.26.cloned.1.call-update) | async-done | bytes 589072 | tf_op jit(solution)/shard_map/reduce_scatter | solution.py:266
  704.0 35.6 %reduce-scatter.24.cloned.1.call-done = bf16[192,1536]{1,0:T(8,128)(2,1)} async-done(((bf16[768,1536]{1,0:T(8,128)(2,1)}), bf16[192,1536]{1,0:T(8,128)(2,1)}) %reduce-scatter.24.cloned.1.call-update) | async-done | bytes 589840 | tf_op jit(solution)/shard_map/reduce_scatter | solution.py:260
  739.6 25.2 %reduce-scatter.22.cloned.1.call-done = bf16[96,767]{1,0:T(8,128)(2,1)} async-done(((bf16[384,767]{1,0:T(8,128)(2,1)}), bf16[96,767]{1,0:T(8,128)(2,1)}) %reduce-scatter.22.cloned.1.call-update) | async-done | bytes 147280 | tf_op jit(solution)/shard_map/reduce_scatter | solution.py:257
  764.9 7.1 copy.87
  771.9 9.1 bitcast_convert_fusion
  781.1 3.7 convert_reduce_fusion
  786.0 6.1 all-reduce
  792.2 18.3 %reduce-scatter.16.cloned.1.call-done = bf16[2,512,767]{2,1,0:T(8,128)(2,1)} async-done(((bf16[2,1024,767]{2,1,0:T(8,128)(2,1)}), bf16[2,512,767]{2,1,0:T(8,128)(2,1)}) %reduce-scatter.16.cloned.1.call-update) | async-done | bytes 1570832 | tf_op jit(solution)/shard_map/reduce_scatter | solution.py:169
  813.5 4.9 copy.90
  818.5 14.5 %reduce-scatter.30.cloned.1.call-done = bf16[96,2]{1,0:T(8,128)(2,1)} async-done(((bf16[384,2]{1,0:T(8,128)(2,1)}), bf16[96,2]{1,0:T(8,128)(2,1)}) %reduce-scatter.30.cloned.1.call-update) | async-done | bytes 400
  833.7 11.8 %all-reduce.3 = (bf16[2,96]{1,0:T(2,128)(2,1)S(1)}, bf16[384]{0:T(512)(128)(2,1)S(1)}) all-reduce(bf16[2,96]{1,0:T(2,128)(2,1)S(1)} %copy.97, bf16[384]{0:T(512)(128)(2,1)S(1)} %dynamic-slice.1), channel_id=1, replica_groups=mesh['dp'=4,'group'=4,'tensor'=2] {'group'}, use_global_device_ids=true, to_apply=%region_29.30 | all-reduce | flops 576 | bytes 2304 | tf_op jit(solution)/shard_map/psum | solution.py:272
  846.7 71.2 %all-reduce.7.cloned.1.call-done = (bf16[3,192,384]{1,2,0:T(8,128)(2,1)}, bf16[96,767]{1,0:T(8,128)(2,1)}, bf16[192,1536]{1,0:T(8,128)(2,1)}, bf16[384,767]{1,0:T(8,128)(2,1)}) async-done(((bf16[3,192,384]{1,2,0:T(8,128)(2,1)}, bf16[96,767]{1,0:T(8,128)(2,1)}, bf16[192,1536]{1,0:T(8,128)(2,1)}, bf16[384,767]{1,0:T(8,128)(2,1)}), (bf16[3,192,384]{1,2,0:T(8,128)(2,1)}, bf16[96,767]{1,0:T(8,128)(2,1)}, ...) | async-done | bytes 1768528 | tf_op jit(solution)/shard_map/psum | solution.py:271
  926.2 36.2 %reduce-scatter.20.cloned.1.call-done = bf16[2,512,768]{2,1,0:T(8,128)(2,1)} async-done(((bf16[2,1024,768]{2,1,0:T(8,128)(2,1)}), bf16[2,512,768]{2,1,0:T(8,128)(2,1)}) %reduce-scatter.20.cloned.1.call-update) | async-done | bytes 1572880 | tf_op jit(solution)/shard_map/reduce_scatter | solution.py:227
  974.7 5.2 reshape.591
  979.9 36.1 %all-reduce.1 = (f32[2,768]{1,0:T(2,128)S(1)}, f32[2,767]{1,0:T(2,128)S(1)}) all-reduce(f32[2,768]{1,0:T(2,128)S(1)} %pad_maximum_fusion.4, f32[2,767]{1,0:T(2,128)S(1)} %pad_maximum_fusion.5), channel_id=1, replica_groups=mesh['dp'=4,'group'=4,'tensor'=2] {'group','tensor'}, use_global_device_ids=true, to_apply=%region_22.23 | all-reduce | flops 3070 | bytes 24560 | tf_op jit(solution)/shard_map/psum | solution.py:13
  1016.0 10.7 %all-reduce.2 = (f32[2,768]{1,0:T(2,128)}, f32[2,767]{1,0:T(2,128)}) all-reduce(f32[2,768]{1,0:T(2,128)S(1)} %get-tuple-element.232, f32[2,767]{1,0:T(2,128)S(1)} %get-tuple-element.233), channel_id=1, replica_groups=mesh['dp'=4,'group'=4,'tensor'=2] {'dp'}, use_global_device_ids=true, to_apply=%region_23.24 | all-reduce | flops 3070 | bytes 24560 | tf_op jit(solution)/shard_map/psum | solution.py:14
  (356 shorter events, 207.3 us)
Async XLA Ops:
  7.2 313.2 %copy-start = (bf16[768,1536]{1,0:T(8,128)(2,1)S(1)}, bf16[768,1536]{1,0:T(8,128)(2,1)}, u32[]{:S(2)}) copy-start(bf16[768,1536]{1,0:T(8,128)(2,1)} %param.21) | copy-start | bytes 7077892
  7.2 69.0 %all-gather.5.cloned.1.call-start = ((), (), s32[]{:S(2)}) async-start(), calls=%async_computation.9 | async-start | bytes 4718592 | tf_op jit(solution)/shard_map/all_gather | solution.py:133
  12.4 5.1 copy-start.58
  18.1 6.8 copy-start.40
  18.1 4.0 copy-start.43
  18.4 6.5 copy-start.31
  24.8 3.5 copy-start.51
  24.9 3.5 copy-start.45
  24.9 3.6 copy-start.60
  28.4 199.0 %reduce-scatter.14.cloned.1.call-start = ((), (), s32[]{:S(2)}) async-start(), calls=%async_computation.10 | async-start | bytes 4718592 | tf_op jit(solution)/shard_map/reduce_scatter | solution.py:154
  124.7 54.4 %copy-start.65 = (bf16[384,767]{1,0:T(8,128)(2,1)S(1)}, bf16[384,767]{1,0:T(8,128)(2,1)}, u32[]{:S(2)}) copy-start(bf16[384,767]{1,0:T(8,128)(2,1)} %param.20) | copy-start | bytes 1767172
  131.4 3.7 copy-start.8
  135.1 3.9 copy-start.2
  146.1 4.5 copy-start.36
  158.4 3.7 copy-start.8
  162.1 3.9 copy-start.2
  173.0 4.5 copy-start.36
  183.9 90.0 %all-gather.9.cloned.1.call-start = ((), (), s32[]{:S(2)}) async-start(), calls=%async_computation.13 | async-start | bytes 4712448 | tf_op jit(solution)/shard_map/all_gather | solution.py:177
  184.7 135.7 %all-gather.7.cloned.1.call-start = ((), (), s32[]{:S(2)}) async-start(), calls=%async_computation.11 | async-start | bytes 4718592 | tf_op jit(solution)/shard_map/all_gather | solution.py:160
  231.7 9.2 copy-start.32
  240.9 3.6 copy-start.56
  244.5 155.1 %reduce-scatter.18.cloned.1.call-start = ((), (), s32[]{:S(2)}) async-start(), calls=%async_computation.14 | async-start | bytes 4718592 | tf_op jit(solution)/shard_map/reduce_scatter | solution.py:191
  320.4 13.9 %copy-start.33 = (bf16[96,8,2,1024]{3,1,2,0:T(8,128)(2,1)S(1)}, bf16[96,8,2,1024]{3,1,2,0:T(8,128)(2,1)}, u32[]{:S(2)}) copy-start(bf16[96,8,2,1024]{3,1,2,0:T(8,128)(2,1)} %copy.101) | copy-start | bytes 9437188
  320.4 13.9 %copy-start.63 = (bf16[1536,767]{1,0:T(8,128)(2,1)S(1)}, bf16[1536,767]{1,0:T(8,128)(2,1)}, u32[]{:S(2)}) copy-start(bf16[1536,767]{1,0:T(8,128)(2,1)} %param.23) | copy-start | bytes 7068676
  349.6 6.4 copy-start.68
  356.0 101.5 %all-gather.11.cloned.1.call-start = ((), (), s32[]{:S(2)}) async-start(), calls=%async_computation.15 | async-start | bytes 4712448 | tf_op jit(solution)/shard_map/all_gather | solution.py:199
  359.6 39.9 %copy-start.11 = (f32[2,512,767]{2,1,0:T(8,128)S(1)}, f32[2,512,767]{2,1,0:T(8,128)}, u32[]{:S(2)}) copy-start(f32[2,512,767]{2,1,0:T(8,128)} %get-tuple-element.245) | copy-start | bytes 9424900
  412.5 263.4 %reduce-scatter.28.cloned.1.call-start = ((), (), s32[]{:S(2)}) async-start(), calls=%async_computation.20 | async-start | bytes 2211840
  467.2 5.5 copy-start.3
  476.7 10.7 %copy-start.5 = (pred[512,1024]{1,0:T(8,128)(4,1)}, pred[512,1024]{1,0:T(8,128)(4,1)S(1)}, u32[]{:S(2)}) copy-start(pred[512,1024]{1,0:T(8,128)(4,1)S(1)} %get-tuple-element.423) | copy-start | bytes 1572868 | tf_op jit(solution)/shard_map/while
  510.9 5.2 copy-start.6
  511.0 5.2 copy-start.9
  524.3 7.0 copy-start.4
  543.4 10.7 %copy-start.5 = (pred[512,1024]{1,0:T(8,128)(4,1)}, pred[512,1024]{1,0:T(8,128)(4,1)S(1)}, u32[]{:S(2)}) copy-start(pred[512,1024]{1,0:T(8,128)(4,1)S(1)} %get-tuple-element.423) | copy-start | bytes 1572868 | tf_op jit(solution)/shard_map/while
  577.6 5.2 copy-start.6
  577.6 5.2 copy-start.9
  591.0 7.0 copy-start.4
  606.5 5.6 copy-start.23
  612.1 6.6 copy-start.27
  624.6 3.5 copy-start.61
  638.7 65.3 %reduce-scatter.26.cloned.1.call-start = ((), (), s32[]{:S(2)}) async-start(), calls=%async_computation.19 | async-start | bytes 2949120 | tf_op jit(solution)/shard_map/reduce_scatter | solution.py:266
  638.7 9.4 copy-start.62
  648.1 91.5 %reduce-scatter.24.cloned.1.call-start = ((), (), s32[]{:S(2)}) async-start(), calls=%async_computation.18 | async-start | bytes 2949120 | tf_op jit(solution)/shard_map/reduce_scatter | solution.py:260
  657.5 3.7 copy-start.35
  657.5 107.2 %reduce-scatter.22.cloned.1.call-start = ((), (), s32[]{:S(2)}) async-start(), calls=%async_computation.17 | async-start | bytes 737280 | tf_op jit(solution)/shard_map/reduce_scatter | solution.py:257
  663.6 147.0 %reduce-scatter.16.cloned.1.call-start = ((), (), s32[]{:S(2)}) async-start(), calls=%async_computation.12 | async-start | bytes 4718592 | tf_op jit(solution)/shard_map/reduce_scatter | solution.py:169
  672.7 160.3 %reduce-scatter.30.cloned.1.call-start = ((), (), s32[]{:S(2)}) async-start(), calls=%async_computation.21 | async-start | bytes 122880
  675.8 242.1 %all-reduce.7.cloned.1.call-start = ((), (), s32[]{:S(2)}) async-start(), calls=%async_computation.22 | async-start | bytes 3833856 | tf_op jit(solution)/shard_map/psum | solution.py:271
  764.8 197.6 %reduce-scatter.20.cloned.1.call-start = ((), (), s32[]{:S(2)}) async-start(), calls=%async_computation.16 | async-start | bytes 4718592 | tf_op jit(solution)/shard_map/reduce_scatter | solution.py:227
  764.9 7.1 copy-start.64
  781.1 3.7 copy-start.67
  781.1 5.0 copy-start.57
  781.1 29.5 %copy-start.12 = (f32[2,512,767]{2,1,0:T(8,128)S(1)}, f32[2,512,767]{2,1,0:T(8,128)}, u32[]{:S(2)}) copy-start(f32[2,512,767]{2,1,0:T(8,128)} %get-tuple-element.245) | copy-start | bytes 9424900
  781.1 29.5 %copy-start.55 = (f32[767]{0:T(1024)S(1)}, f32[767]{0:T(1024)}, u32[]{:S(2)}) copy-start(f32[767]{0:T(1024)} %get-tuple-element.192) | copy-start | bytes 9208
  813.5 4.9 copy-start.53
  813.5 4.9 copy-start.54
  818.4 144.0 %copy-start.10 = (f32[2,512,767]{2,1,0:T(8,128)S(1)}, f32[2,512,767]{2,1,0:T(8,128)}, u32[]{:S(2)}) copy-start(f32[2,512,767]{2,1,0:T(8,128)} %convert_element_type.195) | copy-start | bytes 9424900
  818.4 144.0 %copy-start.41 = (f32[768]{0:T(1024)S(1)}, f32[768]{0:T(1024)}, u32[]{:S(2)}) copy-start(f32[768]{0:T(1024)} %copy-done.40) | copy-start | bytes 9220
  818.4 144.0 %copy-start.46 = (f32[2,512]{1,0:T(2,128)S(1)}, f32[2,512]{1,0:T(2,128)}, u32[]{:S(2)}) copy-start(f32[2,512]{1,0:T(2,128)} %copy-done.45) | copy-start | bytes 12292
  924.0 41.2 %copy-start.50 = (f32[1024]{0:T(1024)S(1)}, f32[1024]{0:T(1024)}, u32[]{:S(2)}) copy-start(f32[1024]{0:T(1024)} %copy-done.49) | copy-start | bytes 12292
  965.1 3.3 copy-start.13
  968.5 3.8 copy-start.17
  968.5 3.8 copy-start.48
  972.2 54.5 %copy-start.1 = (bf16[768,1536]{1,0:T(8,128)(2,1)S(1)}, bf16[768,1536]{1,0:T(8,128)(2,1)}, u32[]{:S(2)}) copy-start(bf16[768,1536]{1,0:T(8,128)(2,1)} %param.21) | copy-start | bytes 7077892
  (37 other events, 76.3 us)
Sparse Core Ops, SparseCore 0:
  28.5 47.6 all-gather.4
  184.0 43.3 reduce-scatter.13
  229.0 44.8 all-gather.8
  275.4 44.9 all-gather.6
  356.2 43.3 reduce-scatter.17
  412.6 44.8 all-gather.10
  638.8 29.3 reduce-scatter.27
  670.9 33.0 reduce-scatter.25
  706.5 33.0 reduce-scatter.23
  742.7 22.0 reduce-scatter.21
  767.1 43.3 reduce-scatter.15
  813.4 19.5 reduce-scatter.29
  836.2 81.6 all-reduce.6
  920.0 42.3 reduce-scatter.19
